TPU v7x, 512 devices: a whole 4x8x8 slice. The times are simulated.
512 devices in a mesh: date: 16 (over z, x_hi), trade: 16 (over y, core), path: 2 (over x_lo).
Axes of the slice: x: 4 (x_hi: 2, x_lo: 2; x = x_hi * 2 + x_lo), y: 8, z: 8, core: 2. Of those that a mesh axis runs over, the one named last changes fastest.
Arguments:
- normals: bfloat16 [32, 64, 8192], P('date', None, ('trade', 'path')), may hold values from -6 to 6
- chol: float32 [64, 64], replicated, as said below
- volatility: float32 [64], replicated, may hold values from 0.5 to 2
- start_state: float32 [64], replicated, may hold values from -3 to 3
- basis_map: float32 [64, 128], replicated, may hold values from -0.75 to 0.75
- basis_bias: float32 [128], replicated, may hold values from -3 to 3
- coef: bfloat16 [128, 16384], P(None, 'trade'), may hold values from -0.5 to 0.5
- maturity: int32 [16384], P('trade'), may hold values from 1 to 32
- netting: int32 [16384], P('trade'), may hold values from 0 to 2047, as said below
Outputs:
- exposure: float32 [32, 2048], P('date', 'trade')
Inputs may be any that keep to these rules, and one draw needn't show every extreme that they name: netting sets are whole within a shard of trades: netting[j] // 128 == j // 1024, and every netting set holds at least one trade. `chol`: lower triangular with a positive diagonal.
All inputs are finite; a program needn't handle non-finite values.
Results may differ from a plain program's by a relative error of at most 0.00035.
Values may be sent and summed in bfloat16 or wider, within the bound.
A program may use at most 64 MiB of HBM per device.

v0:
```python
import jax
import jax.numpy as jnp
from jax import lax
from jax.sharding import PartitionSpec as P

NS_DEV = 128


def entering(array, axis, join, neutral):
    place = lax.axis_index(axis)
    gathered = lax.all_gather(array.astype(jnp.bfloat16), axis)
    state = jnp.zeros_like(array) + jnp.asarray(neutral, array.dtype)

    def one(lap, state):
        return join(state, lax.dynamic_index_in_dim(gathered, lap, 0, False).astype(array.dtype))

    return lax.fori_loop(0, place, one, state)


def add_pair(earlier, later):
    return earlier + later


def local_moves(draws, chol, volatility, date_total):
    scale = volatility * jnp.sqrt(jnp.float32(1.0) / date_total)
    moves = jnp.einsum(
        "fg,tgp->tfp", chol, draws.astype(jnp.float32), precision=lax.Precision.HIGHEST
    )
    return jnp.cumsum(moves * scale[None, :, None], axis=0)


def shards(normals, chol, volatility, start_state, basis_map, basis_bias, coef, maturity, netting):
    date_count, factor_count, path_count = normals.shape
    trade_count = coef.shape[1]
    set_count = trade_count * 0 + NS_DEV
    date_total = date_count * lax.axis_size("date")
    path_total = path_count * lax.axis_size("trade") * lax.axis_size("path")
    first_date = lax.axis_index("date") * date_count
    when = first_date + jnp.arange(date_count, dtype=jnp.int32)
    alive = (when[:, None] < maturity[None, :]).astype(jnp.float32)
    local_set = netting - lax.axis_index("trade") * set_count
    member = (local_set[:, None] == jnp.arange(set_count, dtype=jnp.int32)[None, :]).astype(
        jnp.bfloat16
    )
    own_local = local_moves(normals, chol, volatility, date_total)
    empty = jnp.zeros_like(own_local[-1])
    prior = entering(own_local[-1], "date", add_pair, empty)
    states = start_state[None, :, None] + prior[None] + own_local
    pre = jnp.einsum(
        "tfp,fk->tpk",
        lax.all_gather(states, "trade", axis=2, tiled=True),
        basis_map,
        precision=lax.Precision.HIGHEST,
    )
    basis = jnp.tanh(pre + basis_bias[None, None, :]).astype(jnp.bfloat16)
    value = jnp.einsum("tpk,kj->tpj", basis, coef, preferred_element_type=jnp.float32)
    value = (value * alive[:, None, :]).astype(jnp.bfloat16)
    net = jnp.einsum("tpj,js->tps", value, member, preferred_element_type=jnp.float32)
    total = jnp.sum(jnp.maximum(net, 0.0), axis=1)
    summed = lax.psum(total, "path")
    return summed / path_total


def solution(mesh):
    placed = (
        P("date", None, ("trade", "path")),
        P(),
        P(),
        P(),
        P(),
        P(),
        P(None, "trade"),
        P("trade"),
        P("trade"),
    )
    return jax.shard_map(
        shards, mesh=mesh, in_specs=placed, out_specs=P("date", "trade"), check_vma=False
    )
```

profile of v0, /device:TPU:1, one launch (start us, length us, event | category | flops | bytes accessed | tf_op | source)
XLA Modules:
  0.0 125.8 jit_solution(15111759457493451321)
XLA Ops:
  6.5 0.0 copy-start
  6.5 0.0 copy-start.4
  6.5 0.0 copy-start.3
  6.5 0.0 copy-start.2
  6.5 0.0 copy-start.1
  6.5 0.0 copy-start.5
  6.6 0.0 all-gather.2.cloned.1.call-start
  6.6 0.7 broadcast_multiply_fusion.1
  7.3 1.0 fusion.8
  8.4 0.1 fusion.16
  8.5 43.9 %all_gather.7 = bf16[16,64,256]{2,1,0:T(8,128)(2,1)S(1)} all-gather(bf16[1,64,256]{2,1,0:T(8,128)(2,1)S(1)} %slice.7), channel_id=1, replica_groups=mesh['date'=16,'trade'=16,'path'=2] {'date'}, dimensions={0}, use_global_device_ids=true | all-gather | bytes 557056 | tf_op jit(solution)/shard_map/all_gather | solution.py:11
  52.4 0.0 copy-done.4
  52.4 0.1 broadcast_add_fusion.1
  52.5 0.7 broadcast_add_fusion
  53.2 0.0 all-gather.2.cloned.1.call-update
  53.2 0.0 copy-done.3
  53.2 0.0 copy-done.2
  53.2 0.1 compare_convert_fusion
  53.3 43.9 %all-gather.2.cloned.1.call-done = f32[2,64,4096]{2,1,0:T(8,128)} async-done(((f32[2,64,256]{2,1,0:T(8,128)}), f32[2,64,4096]{2,1,0:T(8,128)}) %all-gather.2.cloned.1.call-update) | async-done | bytes 2097168 | tf_op jit(solution)/shard_map/all_gather | solution.py:51
  97.2 0.0 copy-done.1
  97.2 0.0 copy-done.5
  97.2 8.3 %fusion.6 = bf16[2,4096,128]{2,1,0:T(8,128)(2,1)S(1)} fusion(f32[2,64,4096]{2,1,0:T(8,128)} %all-gather.2.cloned.1.call-done, f32[128]{0:T(128)S(1)} %copy-done.5, f32[64,128]{1,0:T(8,128)S(1)} %copy-done.1), kind=kOutput, calls=%fused_computation.8 | convolution fusion | flops 807403520 | bytes 4227584 | tf_op jit(solution)/shard_map/tfp,fk->tpk/dot_general | solution.py:49
  105.5 0.0 copy-done
  105.5 9.0 %fusion.7 = f32[2,128]{1,0:T(2,128)S(1)} fusion(f32[2,1024]{1,0:T(2,128)S(1)} %compare_convert_fusion, bf16[2,4096,128]{2,1,0:T(8,128)(2,1)S(1)} %fusion.6, bf16[128,1024]{1,0:T(8,128)(2,1)S(1)} %copy-done, s32[1024]{0:T(1024)S(1)} %broadcast_subtract_fusion), kind=kOutput, calls=%fused_computation.9 | convolution fusion | flops 4313972736 | bytes 2372608 | tf_op jit(solution)/shard_map/tpj,js->tps/dot_general | solution.py:58
  114.6 3.8 %psum.7 = f32[2,128]{1,0:T(2,128)S(1)} all-reduce(f32[2,128]{1,0:T(2,128)S(1)} %fusion.7), channel_id=1, replica_groups=mesh['date'=16,'trade'=16,'path'=2] {'path'}, use_global_device_ids=true, to_apply=%region_4.5 | all-reduce | flops 256 | bytes 2048 | tf_op jit(solution)/shard_map/psum | solution.py:60
  118.3 0.6 broadcast_multiply_fusion
  (5 shorter events, 0.0 us)
Async XLA Ops:
  6.5 99.0 %copy-start = (bf16[128,1024]{1,0:T(8,128)(2,1)S(1)}, bf16[128,1024]{1,0:T(8,128)(2,1)}, u32[]{:S(2)}) copy-start(bf16[128,1024]{1,0:T(8,128)(2,1)} %param.17) | copy-start | bytes 786436
  6.5 45.9 %copy-start.4 = (f32[64]{0:T(128)S(1)}, f32[64]{0:T(128)}, u32[]{:S(2)}) copy-start(f32[64]{0:T(128)} %param.14) | copy-start | bytes 772
  6.5 46.7 %copy-start.3 = (s32[1024]{0:T(1024)S(1)}, s32[1024]{0:T(1024)}, u32[]{:S(2)}) copy-start(s32[1024]{0:T(1024)} %param.19) | copy-start | bytes 12292
  6.5 46.7 %copy-start.2 = (s32[1024]{0:T(1024)S(1)}, s32[1024]{0:T(1024)}, u32[]{:S(2)}) copy-start(s32[1024]{0:T(1024)} %param.18) | copy-start | bytes 12292
  6.5 90.6 %copy-start.1 = (f32[64,128]{1,0:T(8,128)S(1)}, f32[64,128]{1,0:T(8,128)}, u32[]{:S(2)}) copy-start(f32[64,128]{1,0:T(8,128)} %param.15) | copy-start | bytes 98308
  6.5 90.6 %copy-start.5 = (f32[128]{0:T(128)S(1)}, f32[128]{0:T(128)}, u32[]{:S(2)}) copy-start(f32[128]{0:T(128)} %param.16) | copy-start | bytes 1540
  6.6 90.6 %all-gather.2.cloned.1.call-start = ((), (), s32[]{:S(2)}) async-start(), calls=%async_computation | async-start | bytes 2228224 | tf_op jit(solution)/shard_map/all_gather | solution.py:51
Sparse Core Ops, SparseCore 0:
  53.3 43.8 all-gather.1
where the time goes:
time: 126 us
  blocking collectives  47.7 us (38%)
  waiting for transfers between devices  43.9 us (35%)
  matrix products  18.4 us (15%)
  between operations  13.5 us (11%)
  other arithmetic  2.22 us (2%)
    all_gather x1, blocking collectives, entering(): gathered = lax.all_gather(array.astype(jnp.bfloat16), axis)  43.9 us
    all_gather x1, waiting for transfers between devices, shards(): lax.all_gather(states, 'trade', axis=2, tiled=True)  43.9 us
    dot_general x1, matrix products, shards(): jnp.einsum('tpj,js->tps', value, member, preferred_element_type=jnp.float32)  9.03 us
    dot_general x1, matrix products, shards(): jnp.einsum('tfp,fk->tpk', lax.all_gather(states, 'trade', axis=2, tiled=T...  8.32 us
    psum x1, blocking collectives, shards(): summed = lax.psum(total, 'path')  3.79 us
  transfers between devices with their start and end apart: 1, of which 1 were waited for; matrix products, arithmetic and copies ran while one was open for 0% of the time, Pallas kernels for 0%

commit v1 on v0

--- a/solution.py
+++ b/solution.py
@@ -48,7 +48,9 @@
     states = start_state[None, :, None] + prior[None] + own_local
     pre = jnp.einsum(
         "tfp,fk->tpk",
-        lax.all_gather(states, "trade", axis=2, tiled=True),
+        jnp.concatenate(
+            lax.all_to_all(jnp.stack([states] * lax.axis_size("trade")), "trade", 0, 0), axis=2
+        ),
         basis_map,
         precision=lax.Precision.HIGHEST,
     )

time: 126 us -> 133 us (1.056)
  starting transfers between devices: 0.04 us -> 14.7 us
  between operations: 13.5 us -> 0.1 us
  waiting for transfers between devices: 43.9 us -> 48.8 us
  local copies, waits for them, and re-layouts: 0.03 us -> 2.36 us
    all_to_all x0 -> x1, waiting for transfers between devices: none -> 48.8 us  [shards(): lax.all_to_all(jnp.stack([states] * lax.axis_size('trade')), 'trade', 0, 0)]
    all_gather x1 -> x0, waiting for transfers between devices: 43.9 us -> none  [shards(): lax.all_gather(states, 'trade', axis=2, tiled=True)]
    all_to_all x0 -> x1, starting transfers between devices: none -> 14.7 us  [shards(): lax.all_to_all(jnp.stack([states] * lax.axis_size('trade')), 'trade', 0, 0)]
    another operation x0 -> x1, local copies, waits for them, and re-layouts: none -> 1.58 us  [shards(): jnp.stack([states] * lax.axis_size('trade'))]
where the time goes in v1:
time: 133 us; the launch traced here: 132 us
  waiting for transfers between devices  48.8 us (37%)
  blocking collectives  47.7 us (36%)
  matrix products  17.2 us (13%)
  starting transfers between devices  14.7 us (11%)
  local copies, waits for them, and re-layouts  2.36 us (2%)
  other arithmetic  1.57 us (1%)
    all_to_all x1, waiting for transfers between devices, shards(): lax.all_to_all(jnp.stack([states] * lax.axis_size('trade')), 'trade', 0, 0)  48.8 us
    all_gather x1, blocking collectives, entering(): gathered = lax.all_gather(array.astype(jnp.bfloat16), axis)  43.9 us
    all_to_all x1, starting transfers between devices, shards(): lax.all_to_all(jnp.stack([states] * lax.axis_size('trade')), 'trade', 0, 0)  14.7 us
    dot_general x1, matrix products, shards(): jnp.einsum('tpj,js->tps', value, member, preferred_element_type=jnp.float32)  9.03 us
    dot_general x1, matrix products, shards(): jnp.einsum('tfp,fk->tpk', jnp.concatenate(lax.all_to_all(jnp.stack([state...  7.17 us
    psum x1, blocking collectives, shards(): summed = lax.psum(total, 'path')  3.79 us
  transfers between devices with their start and end apart: 1, of which 1 were waited for; matrix products, arithmetic and copies ran while one was open for 0% of the time, Pallas kernels for 0%

profile of v1, /device:TPU:1, one launch (start us, length us, event | category | flops | bytes accessed | tf_op | source)
XLA Modules:
  0.0 132.5 jit_solution(4525927525476200663)
XLA Ops:
  0.0 0.0 copy-start
  0.0 0.0 copy-start.4
  0.0 0.7 broadcast_multiply_fusion.1
  0.7 1.0 fusion.8
  1.8 0.1 fusion.16
  1.9 43.9 %all_gather.4 = bf16[16,64,256]{2,1,0:T(8,128)(2,1)S(1)} all-gather(bf16[1,64,256]{2,1,0:T(8,128)(2,1)S(1)} %slice.7), channel_id=1, replica_groups=mesh['date'=16,'trade'=16,'path'=2] {'date'}, dimensions={0}, use_global_device_ids=true | all-gather | bytes 557056 | tf_op jit(solution)/shard_map/all_gather | solution.py:11
  45.8 0.0 copy-done.4
  45.8 0.1 broadcast_add_fusion.1
  45.9 1.6 %stack.2 = f32[16,2,64,256]{3,2,1,0:T(8,128)} broadcast(f32[2,64,256]{2,1,0:T(8,128)S(1)} %broadcast_add_fusion), dimensions={1,2,3} | broadcast | bytes 2228224 | tf_op jit(solution)/shard_map/stack | solution.py:52
  47.5 0.0 copy-start.3
  47.5 0.0 copy-start.2
  47.5 14.7 %all-to-all-start = ((f32[16,2,64,256]{3,2,1,0:T(8,128)}), f32[16,2,64,256]{3,2,1,0:T(8,128)S(1)}, u32[]{:S(2)}, u32[]{:S(2)}) async-start(f32[16,2,64,256]{3,2,1,0:T(8,128)} %stack.2), calls=%async_computation | async-start | bytes 4194304 | tf_op jit(solution)/shard_map/all_to_all | solution.py:52
  62.2 0.0 copy-done.3
  62.2 0.0 copy-done.2
  62.2 0.1 compare_convert_fusion
  62.3 48.8 %all-to-all-done = f32[16,2,64,256]{3,2,1,0:T(8,128)S(1)} async-done(((f32[16,2,64,256]{3,2,1,0:T(8,128)}), f32[16,2,64,256]{3,2,1,0:T(8,128)S(1)}, u32[]{:S(2)}, u32[]{:S(2)}) %all-to-all-start) | async-done | bytes 2097184 | tf_op jit(solution)/shard_map/all_to_all | solution.py:52
  111.1 0.0 copy-start.1
  111.1 0.0 copy-start.5
  111.1 0.2 copy.11
  111.3 0.6 copy-done.1
  111.9 0.0 copy-done.5
  111.9 7.2 %fusion.6 = bf16[2,4096,128]{2,1,0:T(8,128)(2,1)S(1)} fusion(f32[2,64,4096]{2,1,0:T(8,128)S(1)} %bitcast.28, f32[128]{0:T(128)S(1)} %copy-done.5, f32[64,128]{1,0:T(8,128)S(1)} %copy-done.1), kind=kOutput, calls=%fused_computation.8 | convolution fusion | flops 807403520 | bytes 4227584 | tf_op jit(solution)/shard_map/tfp,fk->tpk/dot_general | solution.py:49
  119.1 0.0 copy-done
  119.1 9.0 %fusion.7 = f32[2,128]{1,0:T(2,128)S(1)} fusion(f32[2,1024]{1,0:T(2,128)S(1)} %compare_convert_fusion, bf16[2,4096,128]{2,1,0:T(8,128)(2,1)S(1)} %fusion.6, bf16[128,1024]{1,0:T(8,128)(2,1)S(1)} %copy-done, s32[1024]{0:T(1024)S(1)} %broadcast_subtract_fusion), kind=kOutput, calls=%fused_computation.9 | convolution fusion | flops 4313972736 | bytes 2372608 | tf_op jit(solution)/shard_map/tpj,js->tps/dot_general | solution.py:60
  128.1 3.8 %psum.7 = f32[2,128]{1,0:T(2,128)S(1)} all-reduce(f32[2,128]{1,0:T(2,128)S(1)} %fusion.7), channel_id=1, replica_groups=mesh['date'=16,'trade'=16,'path'=2] {'path'}, use_global_device_ids=true, to_apply=%region_4.5 | all-reduce | flops 256 | bytes 2048 | tf_op jit(solution)/shard_map/psum | solution.py:62
  131.9 0.6 broadcast_multiply_fusion
  (6 shorter events, 0.0 us)
Async XLA Ops:
  0.0 119.1 %copy-start = (bf16[128,1024]{1,0:T(8,128)(2,1)S(1)}, bf16[128,1024]{1,0:T(8,128)(2,1)}, u32[]{:S(2)}) copy-start(bf16[128,1024]{1,0:T(8,128)(2,1)} %param.17) | copy-start | bytes 786436
  0.0 45.8 %copy-start.4 = (f32[64]{0:T(128)S(1)}, f32[64]{0:T(128)}, u32[]{:S(2)}) copy-start(f32[64]{0:T(128)} %param.14) | copy-start | bytes 772
  47.5 14.7 %copy-start.3 = (s32[1024]{0:T(1024)S(1)}, s32[1024]{0:T(1024)}, u32[]{:S(2)}) copy-start(s32[1024]{0:T(1024)} %param.19) | copy-start | bytes 12292
  47.5 14.7 %copy-start.2 = (s32[1024]{0:T(1024)S(1)}, s32[1024]{0:T(1024)}, u32[]{:S(2)}) copy-start(s32[1024]{0:T(1024)} %param.18) | copy-start | bytes 12292
  47.5 63.6 %all-to-all-start = ((f32[16,2,64,256]{3,2,1,0:T(8,128)}), f32[16,2,64,256]{3,2,1,0:T(8,128)S(1)}, u32[]{:S(2)}, u32[]{:S(2)}) async-start(f32[16,2,64,256]{3,2,1,0:T(8,128)} %stack.2), calls=%async_computation | async-start | bytes 4194304 | tf_op jit(solution)/shard_map/all_to_all | solution.py:52
  111.1 0.8 copy-start.1
  111.1 0.8 copy-start.5
